TPU v7x, 32 devices: a whole 2x2x4 slice. The times are simulated.
32 devices in a mesh: wide: 8 (over y, x, core), blk: 4 (over z).
Axes of the slice: x: 2, y: 2, z: 4, core: 2. Of those that a mesh axis runs over, the one named last changes fastest.
Arguments:
- audio: bfloat16 [4096, 1024], P(('wide', 'blk')), may hold values from -1 to 1
- video: bfloat16 [4096, 1024], P(('wide', 'blk')), may hold values from -1 to 1
- owner: int32 [4096, 1], P(('wide', 'blk')), may hold values from 0 to 7; in each aligned block of 128 rows (0 to 127, 128 to 255, ...) at most 32 rows name the same one
- clip_feats: bfloat16 [8192, 1024], P(('wide', 'blk')), may hold values from -24 to 24
- lengths: int32 [8192], P(('wide', 'blk')), may hold values from 1 to 16
- proj_weight: bfloat16 [1024, 1024], replicated, may hold values from -0.1875 to 0.1875
Outputs:
- audio_grad: bfloat16 [4096, 1024], P(('wide', 'blk'))
- feats_grad: bfloat16 [8192, 1024], P(('wide', 'blk'))
- weight_grad: float32 [1024, 1024], P('wide')
Inputs may be any that keep to these rules, and one draw needn't show every extreme that they name: Among the 128 rows of one device, no owner is named more than 32 times, a bound that some block reaches.
All inputs are finite; a program needn't handle non-finite values.
Results may differ from a plain program's by a relative error of at most 0.02.
Values may be sent and summed in bfloat16 or wider, within the bound.
A program may use at most 64 MiB of HBM per device.

v0:
```python
from functools import partial
import jax
import jax.numpy as jnp
from jax import lax
from jax.sharding import PartitionSpec as P


def rows_dot(matrix_a, matrix_b):
    return lax.dot_general(
        matrix_a, matrix_b, (((1,), (1,)), ((), ())), preferred_element_type=jnp.float32
    )


def cols_dot(matrix_a, matrix_b):
    return lax.dot_general(
        matrix_a, matrix_b, (((0,), (0,)), ((), ())), preferred_element_type=jnp.float32
    )


def pair_coeffs(scores, labels, factor):
    return (factor * (jax.nn.sigmoid(4.0 * scores - 2.0) - labels)).astype(jnp.bfloat16)


def shards(audio, video, owner, clip_feats, lengths, proj_weight):
    blocks = lax.axis_size("blk")
    clip_count = audio.shape[0]
    feature_count = audio.shape[1]
    factor = 4.0 / blocks
    row_ids = jnp.arange(clip_count, dtype=jnp.int32)
    offset = lax.axis_index("blk") * clip_count
    gathered = lax.all_gather(video, "blk", axis=0, tiled=True)
    other_ids = jnp.arange(gathered.shape[0], dtype=jnp.int32)
    labels = ((offset + row_ids)[:, None] == other_ids[None, :]).astype(jnp.float32)
    coeffs = pair_coeffs(rows_dot(audio, gathered), labels, factor)
    audio_total = jnp.dot(coeffs, gathered, preferred_element_type=jnp.float32)
    gathered = lax.all_gather(audio, "blk", axis=0, tiled=True)
    other_ids = jnp.arange(gathered.shape[0], dtype=jnp.int32)
    labels = (other_ids[:, None] == (offset + row_ids)[None, :]).astype(jnp.float32)
    coeffs = pair_coeffs(rows_dot(gathered, video), labels, factor)
    video_sum = cols_dot(coeffs, gathered)
    audio_grad = audio_total.astype(jnp.bfloat16)
    video_grad = video_sum.astype(jnp.bfloat16)
    peer_count = lax.axis_size("wide")
    slot_count = clip_feats.shape[0]
    capacity = slot_count // peer_count
    owner_peer = owner[:, 0]
    onehot = (owner_peer[:, None] == jnp.arange(peer_count, dtype=jnp.int32)[None, :]).astype(
        jnp.int32
    )
    slot_rank = jnp.sum((jnp.cumsum(onehot, axis=0) - onehot) * onehot, axis=1)
    target = owner_peer * capacity + slot_rank
    placing = (jnp.arange(slot_count, dtype=jnp.int32)[:, None] == target[None, :]).astype(
        jnp.bfloat16
    )
    packed = jnp.dot(placing, video_grad, preferred_element_type=jnp.float32).astype(jnp.bfloat16)
    packed = packed.reshape(peer_count, capacity, feature_count)
    received = lax.all_to_all(packed, "wide", split_axis=0, concat_axis=0, tiled=True).reshape(
        slot_count, feature_count
    )
    length_scale = lax.rsqrt(lengths.astype(jnp.float32))[:, None]
    pooled = (clip_feats.astype(jnp.float32) * length_scale).astype(jnp.bfloat16)
    preact = jnp.dot(pooled, proj_weight, preferred_element_type=jnp.float32)
    _, pullback = jax.vjp(partial(jax.nn.gelu, approximate=False), preact)
    pre_grad = pullback(received.astype(jnp.float32))[0].astype(jnp.bfloat16)
    feats_grad = (rows_dot(pre_grad, proj_weight) * length_scale).astype(jnp.bfloat16)
    partial_rows = lax.psum_scatter(
        cols_dot(pooled, pre_grad).astype(jnp.bfloat16), "wide", scatter_dimension=0, tiled=True
    )
    weight_grad = lax.psum(partial_rows, "blk").astype(jnp.float32)
    return (audio_grad, feats_grad, weight_grad)


def solution(mesh):
    return jax.shard_map(
        shards,
        mesh=mesh,
        in_specs=(
            P(("wide", "blk"), None),
            P(("wide", "blk"), None),
            P(("wide", "blk"), None),
            P(("wide", "blk"), None),
            P(("wide", "blk")),
            P(),
        ),
        out_specs=(P(("wide", "blk"), None), P(("wide", "blk"), None), P("wide", None)),
        check_vma=False,
    )
```

profile of v0, /device:TPU:0, one launch (start us, length us, event | category | flops | bytes accessed | tf_op | source)
XLA Modules:
  0.0 167.4 jit_solution(1915806834253951210)
XLA Ops:
  7.2 0.0 copy-start
  7.2 0.0 all-gather.5.cloned.1.call-start
  7.2 0.7 all-gather.5.cloned.1.call-update
  7.9 0.7 fusion.37
  8.7 0.2 reduce_window_sum.11
  8.8 0.8 select_reduce_fusion
  9.7 0.7 multiply_add_fusion
  10.3 30.0 %all-gather.5.cloned.1.call-done = bf16[512,1024]{1,0:T(8,128)(2,1)} async-done(((bf16[128,1024]{1,0:T(8,128)(2,1)}), bf16[512,1024]{1,0:T(8,128)(2,1)}) %all-gather.5.cloned.1.call-update) | async-done | bytes 1048592 | tf_op jit(solution)/shard_map/all_gather | solution.py:36
  40.3 1.8 %fusion.14 = bf16[512,128]{1,0:T(8,128)(2,1)S(1)} fusion(bf16[512,1024]{1,0:T(8,128)(2,1)} %all-gather.5.cloned.1.call-done, bf16[128,1024]{1,0:T(8,128)(2,1)} %param.7, s32[128]{0:T(128)S(1)} %iota_add_fusion), kind=kOutput, calls=%fused_computation.24 | convolution fusion | flops 134807552 | bytes 1442304 | tf_op jit(solution)/shard_map/dot_general | solution.py:9
  42.1 0.0 copy-start.6
  42.1 1.4 convolution_convert_fusion.1
  43.5 3.7 %all-to-all-start = ((bf16[8,32,1024]{2,1,0:T(8,128)(2,1)}), bf16[8,32,1024]{2,1,0:T(8,128)(2,1)S(1)}, u32[]{:S(2)}, u32[]{:S(2)}) async-start(bf16[8,32,1024]{2,1,0:T(8,128)(2,1)} %bitcast.1), calls=%async_computation | async-start | bytes 1048576 | tf_op jit(solution)/shard_map/all_to_all | solution.py:57
  47.2 0.0 all-gather.3.cloned.1.call-start
  47.2 0.7 all-gather.3.cloned.1.call-update
  47.9 0.0 reduce-scatter.2.cloned.1.call-start
  48.0 0.0 copy-start.2
  48.0 8.9 %all-to-all-done = bf16[8,32,1024]{2,1,0:T(8,128)(2,1)S(1)} async-done(((bf16[8,32,1024]{2,1,0:T(8,128)(2,1)}), bf16[8,32,1024]{2,1,0:T(8,128)(2,1)S(1)}, u32[]{:S(2)}, u32[]{:S(2)}) %all-to-all-start) | async-done | bytes 524320 | tf_op jit(solution)/shard_map/all_to_all | solution.py:57
  56.9 0.0 copy-done
  56.9 4.2 %fusion.20 = bf16[256,1024]{1,0:T(8,128)(2,1)S(1)} fusion(bf16[8,32,1024]{2,1,0:T(8,128)(2,1)S(1)} %all-to-all-done, bf16[1024,1024]{1,0:T(8,128)(2,1)S(1)} %copy-done, bf16[256,1024]{1,0:T(8,128)(2,1)} %param.9, f32[256]{0:T(256)S(1)} %convert_rsqrt_fusion), kind=kOutput, calls=%fused_computation.30 | convolution fusion | flops 556793856 | bytes 3671040 | tf_op jit(solution)/shard_map/dot_general | solution.py:62
  61.1 0.0 copy-start.3
  61.1 0.8 copy-done.3
  61.9 2.2 %convolution_convert_fusion = bf16[1024,1024]{1,0:T(8,128)(2,1)} fusion(bf16[256,1024]{1,0:T(8,128)(2,1)S(1)} %fusion.20, bf16[256,1024]{1,0:T(8,128)(2,1)S(1)} %copy-done.2, f32[256]{0:T(256)S(1)} %convert_rsqrt_fusion), kind=kOutput, calls=%fused_computation | convolution fusion | flops 538705920 | bytes 3146752 | tf_op jit(solution)/shard_map/dot_general | solution.py:15
  64.1 0.0 reduce-scatter.2.cloned.1.call-update
  64.1 0.0 copy-start.4
  64.1 0.0 all-reduce.2.cloned.1.call-start
  64.2 13.3 %all-gather.3.cloned.1.call-done = bf16[512,1024]{1,0:T(8,128)(2,1)} async-done(((bf16[128,1024]{1,0:T(8,128)(2,1)}), bf16[512,1024]{1,0:T(8,128)(2,1)}) %all-gather.3.cloned.1.call-update) | async-done | bytes 1048592 | tf_op jit(solution)/shard_map/all_gather | solution.py:31
  77.5 3.1 %convolution_convert_fusion.3 = bf16[128,1024]{1,0:T(8,128)(2,1)} fusion(bf16[512,1024]{1,0:T(8,128)(2,1)} %all-gather.3.cloned.1.call-done, bf16[128,1024]{1,0:T(8,128)(2,1)S(1)} %copy-done.5, s32[128]{0:T(128)S(1)} %iota_add_fusion), kind=kOutput, calls=%fused_computation.8 | convolution fusion | flops 269156352 | bytes 1573376 | tf_op jit(solution)/shard_map/dot_general | solution.py:35
  80.5 40.8 %reduce-scatter.2.cloned.1.call-done = bf16[128,1024]{1,0:T(8,128)(2,1)} async-done(((bf16[1024,1024]{1,0:T(8,128)(2,1)}), bf16[128,1024]{1,0:T(8,128)(2,1)}) %reduce-scatter.2.cloned.1.call-update) | async-done | bytes 262160 | tf_op jit(solution)/shard_map/reduce_scatter | solution.py:66
  121.3 0.0 all-reduce.2.cloned.1.call-update
  121.3 1.6 fusion
  122.9 36.2 %all-reduce.2.cloned.1.call-done = bf16[128,1024]{1,0:T(8,128)(2,1)} async-done(((bf16[128,1024]{1,0:T(8,128)(2,1)}), bf16[128,1024]{1,0:T(8,128)(2,1)}) %all-reduce.2.cloned.1.call-update) | async-done | bytes 262160 | tf_op jit(solution)/shard_map/psum | solution.py:69
  159.1 1.8 %convert_element_type.68 = f32[128,1024]{1,0:T(8,128)} convert(bf16[128,1024]{1,0:T(8,128)(2,1)} %all-reduce.2.cloned.1.call-done) | non-fusion elementwise | flops 131072 | bytes 786432 | tf_op jit(solution)/shard_map/convert_element_type | solution.py:69
  (9 shorter events, 0.0 us)
Async XLA Ops:
  7.2 49.7 %copy-start = (bf16[1024,1024]{1,0:T(8,128)(2,1)S(1)}, bf16[1024,1024]{1,0:T(8,128)(2,1)}, u32[]{:S(2)}) copy-start(bf16[1024,1024]{1,0:T(8,128)(2,1)} %param.11) | copy-start | bytes 6291460
  7.2 33.1 %all-gather.5.cloned.1.call-start = ((), (), s32[]{:S(2)}) async-start(), calls=%async_computation.3 | async-start | bytes 1310720 | tf_op jit(solution)/shard_map/all_gather | solution.py:36
  40.3 1.8 %copy-start.1 = (bf16[512,1024]{1,0:T(8,128)(2,1)S(1)}, bf16[512,1024]{1,0:T(8,128)(2,1)}, u32[]{:S(2)}) copy-start(bf16[512,1024]{1,0:T(8,128)(2,1)} %all-gather.5.cloned.1.call-done) | copy-start | bytes 3145732
  42.1 5.8 %copy-start.6 = (s32[256]{0:T(256)S(1)}, s32[256]{0:T(256)}, u32[]{:S(2)}) copy-start(s32[256]{0:T(256)} %param.10) | copy-start | bytes 3076
  43.5 13.4 %all-to-all-start = ((bf16[8,32,1024]{2,1,0:T(8,128)(2,1)}), bf16[8,32,1024]{2,1,0:T(8,128)(2,1)S(1)}, u32[]{:S(2)}, u32[]{:S(2)}) async-start(bf16[8,32,1024]{2,1,0:T(8,128)(2,1)} %bitcast.1), calls=%async_computation | async-start | bytes 1048576 | tf_op jit(solution)/shard_map/all_to_all | solution.py:57
  47.2 30.3 %all-gather.3.cloned.1.call-start = ((), (), s32[]{:S(2)}) async-start(), calls=%async_computation.2 | async-start | bytes 1310720 | tf_op jit(solution)/shard_map/all_gather | solution.py:31
  47.9 73.4 %reduce-scatter.2.cloned.1.call-start = ((), (), s32[]{:S(2)}) async-start(), calls=%async_computation.4 | async-start | bytes 2359296 | tf_op jit(solution)/shard_map/reduce_scatter | solution.py:66
  48.0 13.9 %copy-start.2 = (bf16[256,1024]{1,0:T(8,128)(2,1)S(1)}, bf16[256,1024]{1,0:T(8,128)(2,1)}, u32[]{:S(2)}) copy-start(bf16[256,1024]{1,0:T(8,128)(2,1)} %param.9) | copy-start | bytes 1572868
  61.1 0.8 copy-start.3
  61.9 15.6 %copy-start.5 = (bf16[128,1024]{1,0:T(8,128)(2,1)S(1)}, bf16[128,1024]{1,0:T(8,128)(2,1)}, u32[]{:S(2)}) copy-start(bf16[128,1024]{1,0:T(8,128)(2,1)} %param.6) | copy-start | bytes 786436
  64.1 57.2 %copy-start.4 = (bf16[256,1024]{1,0:T(8,128)(2,1)S(1)}, bf16[256,1024]{1,0:T(8,128)(2,1)}, u32[]{:S(2)}) copy-start(bf16[256,1024]{1,0:T(8,128)(2,1)} %copy-done.3) | copy-start | bytes 1572868
  64.1 95.0 %all-reduce.2.cloned.1.call-start = ((), (), s32[]{:S(2)}) async-start(), calls=%async_computation.5 | async-start | bytes 524288 | tf_op jit(solution)/shard_map/psum | solution.py:69
Sparse Core Ops, SparseCore 0:
  9.6 30.6 all-gather.4
  49.5 27.8 all-gather.2
  80.7 40.4 reduce-scatter.1
  123.5 35.5 all-reduce.1
where the time goes:
time: 168 us; the launch traced here: 167 us
  waiting for transfers between devices  131 us (78%)
  matrix products  14.2 us (8%)
  between operations  13.9 us (8%)
  other arithmetic  4.2 us (2%)
  starting transfers between devices  3.81 us (2%)
    reduce_scatter x1, waiting for transfers between devices, shards(): lax.psum_scatter(cols_dot(pooled, pre_grad).astype(jnp.bfloat16), 'wide',...  40.8 us
    psum x1, waiting for transfers between devices, shards(): weight_grad = lax.psum(partial_rows, 'blk').astype(jnp.float32)  36.2 us
    all_gather x1, waiting for transfers between devices, shards(): gathered = lax.all_gather(audio, 'blk', axis=0, tiled=True)  30 us
    all_gather x1, waiting for transfers between devices, shards(): gathered = lax.all_gather(video, 'blk', axis=0, tiled=True)  13.3 us
    all_to_all x1, waiting for transfers between devices, shards(): lax.all_to_all(packed, 'wide', split_axis=0, concat_axis=0, tiled=True)  8.88 us
    dot_general x1, matrix products, shards(): preact = jnp.dot(pooled, proj_weight, preferred_element_type=jnp.float32)  4.22 us
    all_to_all x1, starting transfers between devices, shards(): lax.all_to_all(packed, 'wide', split_axis=0, concat_axis=0, tiled=True)  3.65 us
    dot_general x2, matrix products, rows_dot(): lax.dot_general(matrix_a, matrix_b, (((1,), (1,)), ((), ())), preferred_e...  3.41 us
  transfers between devices with their start and end apart: 5, of which 5 were waited for; matrix products, arithmetic and copies ran while one was open for 8% of the time, Pallas kernels for 0%

commit v1 on v0

--- a/solution.py
+++ b/solution.py
@@ -28,7 +28,12 @@
     factor = 4.0 / blocks
     row_ids = jnp.arange(clip_count, dtype=jnp.int32)
     offset = lax.axis_index("blk") * clip_count
-    gathered = lax.all_gather(video, "blk", axis=0, tiled=True)
+    ring = [video]
+    for hop in range(3):
+        ring.append(lax.ppermute(ring[-1], "blk", [(dev, (dev + 1) % 4) for dev in range(4)]))
+    gathered = jnp.roll(
+        jnp.concatenate(ring[::-1], axis=0), (lax.axis_index("blk") + 1) * ring[0].shape[0], axis=0
+    )
     other_ids = jnp.arange(gathered.shape[0], dtype=jnp.int32)
     labels = ((offset + row_ids)[:, None] == other_ids[None, :]).astype(jnp.float32)
     coeffs = pair_coeffs(rows_dot(audio, gathered), labels, factor)

time: 168 us -> 149 us (0.89)
  waiting for transfers between devices: 131 us -> 105 us
  local copies, waits for them, and re-layouts: 0.82 us -> 6.58 us
    reduce_scatter x1, waiting for transfers between devices: 40.8 us -> 4.92 us  [shards(): lax.psum_scatter(cols_dot(pooled, pre_grad).astype(jnp.bfloat16), 'wide',...]
    ppermute x0 -> x3, waiting for transfers between devices: none -> 23.4 us  [shards(): lax.ppermute(ring[-1], 'blk', [(dev, (dev + 1) % 4) for dev in range(4)])]
    all_gather x1 -> x0, waiting for transfers between devices: 13.3 us -> none  [shards(): gathered = lax.all_gather(video, 'blk', axis=0, tiled=True)]
    unnamed x14 -> x23, local copies, waits for them, and re-layouts: 0.82 us -> 5.87 us
  transfers between devices with their start and end apart: 5 -> 7, of which waited for: 5 -> 7; matrix products, arithmetic and copies ran while one was open for 8% -> 9% of each run, Pallas kernels for 0% -> 0%
where the time goes in v1:
time: 149 us
  waiting for transfers between devices  105 us (70%)
  matrix products  14.3 us (10%)
  between operations  13.9 us (9%)
  local copies, waits for them, and re-layouts  6.58 us (4%)
  starting transfers between devices  5.27 us (4%)
  other arithmetic  4.2 us (3%)
    psum x1, waiting for transfers between devices, shards(): weight_grad = lax.psum(partial_rows, 'blk').astype(jnp.float32)  36.2 us
    all_gather x1, waiting for transfers between devices, shards(): gathered = lax.all_gather(audio, 'blk', axis=0, tiled=True)  30 us
    ppermute x3, waiting for transfers between devices, shards(): lax.ppermute(ring[-1], 'blk', [(dev, (dev + 1) % 4) for dev in range(4)])  23.4 us
    all_to_all x1, waiting for transfers between devices, shards(): lax.all_to_all(packed, 'wide', split_axis=0, concat_axis=0, tiled=True)  9.63 us
    unnamed x23, local copies, waits for them, and re-layouts  5.87 us
    reduce_scatter x1, waiting for transfers between devices, shards(): lax.psum_scatter(cols_dot(pooled, pre_grad).astype(jnp.bfloat16), 'wide',...  4.92 us
    dot_general x1, matrix products, shards(): preact = jnp.dot(pooled, proj_weight, preferred_element_type=jnp.float32)  4.2 us
    all_to_all x1, starting transfers between devices, shards(): lax.all_to_all(packed, 'wide', split_axis=0, concat_axis=0, tiled=True)  3.65 us
  transfers between devices with their start and end apart: 7, of which 7 were waited for; matrix products, arithmetic and copies ran while one was open for 9% of the time, Pallas kernels for 0%

profile of v1, /device:TPU:0, one launch (start us, length us, event | category | flops | bytes accessed | tf_op | source)
XLA Modules:
  0.0 149.0 jit_solution(14570207833803825032)
XLA Ops:
  7.2 0.0 all-gather.2.cloned.1.call-start
  7.2 0.7 all-gather.2.cloned.1.call-update
  7.9 0.7 fusion.40
  8.7 0.2 reduce_window_sum.11
  8.8 0.8 select_reduce_fusion
  9.7 0.7 multiply_add_fusion
  10.3 30.0 %all-gather.2.cloned.1.call-done = bf16[512,1024]{1,0:T(8,128)(2,1)} async-done(((bf16[128,1024]{1,0:T(8,128)(2,1)}), bf16[512,1024]{1,0:T(8,128)(2,1)}) %all-gather.2.cloned.1.call-update) | async-done | bytes 1048592 | tf_op jit(solution)/shard_map/all_gather | solution.py:41
  40.3 1.8 %fusion.15 = bf16[512,128]{1,0:T(8,128)(2,1)S(1)} fusion(bf16[512,1024]{1,0:T(8,128)(2,1)} %all-gather.2.cloned.1.call-done, bf16[128,1024]{1,0:T(8,128)(2,1)} %param.7, s32[128]{0:T(128)S(1)} %iota_add_fusion), kind=kOutput, calls=%fused_computation.25 | convolution fusion | flops 134807552 | bytes 1442304 | tf_op jit(solution)/shard_map/dot_general | solution.py:9
  42.1 1.4 convolution_convert_fusion.1
  43.5 3.7 %all-to-all-start = ((bf16[8,32,1024]{2,1,0:T(8,128)(2,1)}), bf16[8,32,1024]{2,1,0:T(8,128)(2,1)S(1)}, u32[]{:S(2)}, u32[]{:S(2)}) async-start(bf16[8,32,1024]{2,1,0:T(8,128)(2,1)} %bitcast.2), calls=%async_computation | async-start | bytes 1048576 | tf_op jit(solution)/shard_map/all_to_all | solution.py:62
  47.2 9.6 %all-to-all-done = bf16[8,32,1024]{2,1,0:T(8,128)(2,1)S(1)} async-done(((bf16[8,32,1024]{2,1,0:T(8,128)(2,1)}), bf16[8,32,1024]{2,1,0:T(8,128)(2,1)S(1)}, u32[]{:S(2)}, u32[]{:S(2)}) %all-to-all-start) | async-done | bytes 524320 | tf_op jit(solution)/shard_map/all_to_all | solution.py:62
  56.9 4.2 %fusion.21 = bf16[256,1024]{1,0:T(8,128)(2,1)S(1)} fusion(bf16[8,32,1024]{2,1,0:T(8,128)(2,1)S(1)} %all-to-all-done, bf16[1024,1024]{1,0:T(8,128)(2,1)S(1)} %copy-done, bf16[256,1024]{1,0:T(8,128)(2,1)} %param.9, f32[256]{0:T(256)S(1)} %convert_rsqrt_fusion), kind=kOutput, calls=%fused_computation.31 | convolution fusion | flops 556793856 | bytes 3671040 | tf_op jit(solution)/shard_map/dot_general | solution.py:67
  61.1 0.8 copy-done.4
  61.9 2.2 %convolution_convert_fusion = bf16[1024,1024]{1,0:T(8,128)(2,1)} fusion(bf16[256,1024]{1,0:T(8,128)(2,1)S(1)} %fusion.21, bf16[256,1024]{1,0:T(8,128)(2,1)S(1)} %copy-done.3, f32[256]{0:T(256)S(1)} %convert_rsqrt_fusion), kind=kOutput, calls=%fused_computation | convolution fusion | flops 538705920 | bytes 3146752 | tf_op jit(solution)/shard_map/dot_general | solution.py:15
  64.1 0.0 all-reduce.2.cloned.1.call-start
  64.1 1.5 %collective-permute-start = (bf16[128,1024]{1,0:T(8,128)(2,1)S(1)}, bf16[128,1024]{1,0:T(8,128)(2,1)S(1)}, u32[]{:S(2)}, u32[]{:S(2)}) collective-permute-start(bf16[128,1024]{1,0:T(8,128)(2,1)S(1)} %copy-done.2), channel_id=1, source_target_pairs={{0,1},{1,2},{2,3},{3,0},{4,5},{5,6},{6,7},{7,4},{8,9},{9,10},{10,1... | collective-permute-start | bytes 786440 | tf_op jit(solution)/shard_map/ppermute | solution.py:33
  65.6 6.7 %collective-permute-done = bf16[128,1024]{1,0:T(8,128)(2,1)S(1)} collective-permute-done((bf16[128,1024]{1,0:T(8,128)(2,1)S(1)}, bf16[128,1024]{1,0:T(8,128)(2,1)S(1)}, u32[]{:S(2)}, u32[]{:S(2)}) %collective-permute-start) | collective-permute-done | bytes 262176 | tf_op jit(solution)/shard_map/ppermute | solution.py:33
  72.4 8.5 %collective-permute-done.1 = bf16[128,1024]{1,0:T(8,128)(2,1)S(1)} collective-permute-done((bf16[128,1024]{1,0:T(8,128)(2,1)S(1)}, bf16[128,1024]{1,0:T(8,128)(2,1)S(1)}, u32[]{:S(2)}, u32[]{:S(2)}) %collective-permute-start.1) | collective-permute-done | bytes 262176 | tf_op jit(solution)/shard_map/ppermute | solution.py:33
  80.9 8.2 %collective-permute-done.2 = bf16[128,1024]{1,0:T(8,128)(2,1)S(1)} collective-permute-done((bf16[128,1024]{1,0:T(8,128)(2,1)S(1)}, bf16[128,1024]{1,0:T(8,128)(2,1)S(1)}, u32[]{:S(2)}, u32[]{:S(2)}) %collective-permute-start.2) | collective-permute-done | bytes 262176 | tf_op jit(solution)/shard_map/ppermute | solution.py:33
  89.0 0.7 constant_dynamic-update-slice_fusion.7
  89.7 0.7 constant_dynamic-update-slice_fusion.6
  90.5 0.7 constant_dynamic-update-slice_fusion.5
  91.2 0.7 constant_dynamic-update-slice_fusion.4
  91.9 0.7 constant_dynamic-update-slice_fusion.3
  92.6 0.7 constant_dynamic-update-slice_fusion.2
  93.3 0.7 constant_dynamic-update-slice_fusion.1
  94.1 0.7 constant_dynamic-update-slice_fusion
  94.8 3.2 %convolution_convert_fusion.3 = bf16[128,1024]{1,0:T(8,128)(2,1)} fusion(bf16[128,1024]{1,0:T(8,128)(2,1)S(1)} %copy-done.6, bf16[1024,1024]{1,0:T(8,128)(2,1)} %constant_dynamic-update-slice_fusion, s32[]{:T(128)S(6)} %select_n.14, s32[128]{0:T(128)S(1)} %iota_add_fusion), kind=kOutput, calls=%fused_computation.8 | convolution fusion | flops 269156352 | bytes 2622976 | tf_op jit(solution)/shard_map/dot_general | solution.py:40
  98.0 4.9 %reduce-scatter.2.cloned.1.call-done = bf16[128,1024]{1,0:T(8,128)(2,1)} async-done(((bf16[1024,1024]{1,0:T(8,128)(2,1)}), bf16[128,1024]{1,0:T(8,128)(2,1)}) %reduce-scatter.2.cloned.1.call-update) | async-done | bytes 262160 | tf_op jit(solution)/shard_map/reduce_scatter | solution.py:71
  102.9 1.5 %fusion = bf16[256,1024]{1,0:T(8,128)(2,1)} fusion(bf16[256,1024]{1,0:T(8,128)(2,1)S(1)} %copy-done.5, bf16[1024,1024]{1,0:T(8,128)(2,1)S(1)} %copy-done, f32[256]{0:T(256)S(1)} %convert_rsqrt_fusion), kind=kOutput, calls=%fused_computation.5 | convolution fusion | flops 537395200 | bytes 3146752 | tf_op jit(solution)/shard_map/dot_general | solution.py:9
  104.5 36.2 %all-reduce.2.cloned.1.call-done = bf16[128,1024]{1,0:T(8,128)(2,1)} async-done(((bf16[128,1024]{1,0:T(8,128)(2,1)}), bf16[128,1024]{1,0:T(8,128)(2,1)}) %all-reduce.2.cloned.1.call-update) | async-done | bytes 262160 | tf_op jit(solution)/shard_map/psum | solution.py:74
  140.7 1.8 %convert_element_type.68 = f32[128,1024]{1,0:T(8,128)} convert(bf16[128,1024]{1,0:T(8,128)(2,1)} %all-reduce.2.cloned.1.call-done) | non-fusion elementwise | flops 131072 | bytes 786432 | tf_op jit(solution)/shard_map/convert_element_type | solution.py:74
  (22 shorter events, 0.1 us)
Async XLA Ops:
  7.2 49.7 %copy-start = (bf16[1024,1024]{1,0:T(8,128)(2,1)S(1)}, bf16[1024,1024]{1,0:T(8,128)(2,1)}, u32[]{:S(2)}) copy-start(bf16[1024,1024]{1,0:T(8,128)(2,1)} %param.11) | copy-start | bytes 6291460
  7.2 33.1 %all-gather.2.cloned.1.call-start = ((), (), s32[]{:S(2)}) async-start(), calls=%async_computation.2 | async-start | bytes 1310720 | tf_op jit(solution)/shard_map/all_gather | solution.py:41
  10.3 36.9 %copy-start.7 = (s32[256]{0:T(256)S(1)}, s32[256]{0:T(256)}, u32[]{:S(2)}) copy-start(s32[256]{0:T(256)} %param.10) | copy-start | bytes 3076
  40.3 1.8 %copy-start.1 = (bf16[512,1024]{1,0:T(8,128)(2,1)S(1)}, bf16[512,1024]{1,0:T(8,128)(2,1)}, u32[]{:S(2)}) copy-start(bf16[512,1024]{1,0:T(8,128)(2,1)} %all-gather.2.cloned.1.call-done) | copy-start | bytes 3145732
  43.5 13.4 %all-to-all-start = ((bf16[8,32,1024]{2,1,0:T(8,128)(2,1)}), bf16[8,32,1024]{2,1,0:T(8,128)(2,1)S(1)}, u32[]{:S(2)}, u32[]{:S(2)}) async-start(bf16[8,32,1024]{2,1,0:T(8,128)(2,1)} %bitcast.2), calls=%async_computation | async-start | bytes 1048576 | tf_op jit(solution)/shard_map/all_to_all | solution.py:62
  47.1 55.7 %reduce-scatter.2.cloned.1.call-start = ((), (), s32[]{:S(2)}) async-start(), calls=%async_computation.3 | async-start | bytes 2359296 | tf_op jit(solution)/shard_map/reduce_scatter | solution.py:71
  47.2 14.6 %copy-start.3 = (bf16[256,1024]{1,0:T(8,128)(2,1)S(1)}, bf16[256,1024]{1,0:T(8,128)(2,1)}, u32[]{:S(2)}) copy-start(bf16[256,1024]{1,0:T(8,128)(2,1)} %param.9) | copy-start | bytes 1572868
  61.1 0.8 copy-start.4
  61.9 2.3 %copy-start.2 = (bf16[128,1024]{1,0:T(8,128)(2,1)S(1)}, bf16[128,1024]{1,0:T(8,128)(2,1)}, u32[]{:S(2)}) copy-start(bf16[128,1024]{1,0:T(8,128)(2,1)} %param.7) | copy-start | bytes 786436
  64.1 76.6 %all-reduce.2.cloned.1.call-start = ((), (), s32[]{:S(2)}) async-start(), calls=%async_computation.4 | async-start | bytes 524288 | tf_op jit(solution)/shard_map/psum | solution.py:74
  64.1 8.2 %collective-permute-start = (bf16[128,1024]{1,0:T(8,128)(2,1)S(1)}, bf16[128,1024]{1,0:T(8,128)(2,1)S(1)}, u32[]{:S(2)}, u32[]{:S(2)}) collective-permute-start(bf16[128,1024]{1,0:T(8,128)(2,1)S(1)} %copy-done.2), channel_id=1, source_target_pairs={{0,1},{1,2},{2,3},{3,0},{4,5},{5,6},{6,7},{7,4},{8,9},{9,10},{10,1... | collective-permute-start | bytes 786440 | tf_op jit(solution)/shard_map/ppermute | solution.py:33
  72.4 8.5 %collective-permute-start.1 = (bf16[128,1024]{1,0:T(8,128)(2,1)S(1)}, bf16[128,1024]{1,0:T(8,128)(2,1)S(1)}, u32[]{:S(2)}, u32[]{:S(2)}) collective-permute-start(bf16[128,1024]{1,0:T(8,128)(2,1)S(1)} %collective-permute-done), channel_id=1, source_target_pairs={{0,1},{1,2},{2,3},{3,0},{4,5},{5,6},{6,7},{7,4},{8,9},{9,10},{10,1... | collective-permute-start | bytes 786440 | tf_op jit(solution)/shard_map/ppermute | solution.py:33
  80.9 8.2 %collective-permute-start.2 = (bf16[128,1024]{1,0:T(8,128)(2,1)S(1)}, bf16[128,1024]{1,0:T(8,128)(2,1)S(1)}, u32[]{:S(2)}, u32[]{:S(2)}) collective-permute-start(bf16[128,1024]{1,0:T(8,128)(2,1)S(1)} %collective-permute-done.1), channel_id=1, source_target_pairs={{0,1},{1,2},{2,3},{3,0},{4,5},{5,6},{6,7},{7,4},{8,9},{9,10},{10,1... | collective-permute-start | bytes 786440 | tf_op jit(solution)/shard_map/ppermute | solution.py:33
  80.9 13.9 %copy-start.6 = (bf16[128,1024]{1,0:T(8,128)(2,1)S(1)}, bf16[128,1024]{1,0:T(8,128)(2,1)}, u32[]{:S(2)}) copy-start(bf16[128,1024]{1,0:T(8,128)(2,1)} %param.6) | copy-start | bytes 786436
  94.1 8.8 %copy-start.5 = (bf16[256,1024]{1,0:T(8,128)(2,1)S(1)}, bf16[256,1024]{1,0:T(8,128)(2,1)}, u32[]{:S(2)}) copy-start(bf16[256,1024]{1,0:T(8,128)(2,1)} %copy-done.4) | copy-start | bytes 1572868
Sparse Core Ops, SparseCore 0:
  9.6 30.6 all-gather.1
  64.2 38.6 reduce-scatter.1
  105.2 35.4 all-reduce.1
